TPU v7x, 256 devices: a whole 4x4x8 slice. The times are simulated.
256 devices in a mesh: row: 32 (over z, x_hi, core), col: 8 (over x_lo, y).
Axes of the slice: x: 4 (x_hi: 2, x_lo: 2; x = x_hi * 2 + x_lo), y: 4, z: 8, core: 2. Of those that a mesh axis runs over, the one named last changes fastest.
Arguments:
- tokens: bfloat16 [2048, 12288], P('col', 'row'), may hold values from -6 to 6
- weight: bfloat16 [12288, 24576], P('row', 'col'), may hold values from -0.0546875 to 0.0546875
- pre_act: bfloat16 [2048, 24576], P('row', 'col'), may hold values from -6 to 6
- out_grad: bfloat16 [2048, 24576], P('row', 'col'), may hold values from -6 to 6
Outputs:
- input_grad: bfloat16 [2048, 12288], P('col', 'row')
- weight_grad: bfloat16 [12288, 24576], P('row', 'col')
- left_stats: bfloat16 [12288, 24576], P('row', 'col')
- right_stats: bfloat16 [12288, 24576], P('row', 'col')
All inputs are finite; a program needn't handle non-finite values.
Results may differ from a plain program's by a relative error of at most 0.0054.
Values may be sent and summed in bfloat16 or wider, within the bound.
A program may use at most 128 MiB of HBM per device.

v0:
```python
import math
import jax
import jax.numpy as jnp
from jax import lax
from jax.sharding import PartitionSpec as P

BLOCK = 384


def gelu_slope(value):
    coeff = math.sqrt(2.0 / math.pi)
    inner = coeff * (value + 0.044715 * value * value * value)
    tanh_u = jnp.tanh(inner)
    return 0.5 * (1.0 + tanh_u) + 0.5 * value * (1.0 - tanh_u * tanh_u) * coeff * (
        1.0 + 3.0 * 0.044715 * value * value
    )


def on_device(tokens, weight, pre_act, out_grad):
    x_all = lax.all_gather(tokens, "col", axis=0, tiled=True)
    num_tokens = x_all.shape[0]
    rows_here = weight.shape[0]
    cols_here = weight.shape[1]
    hidden_grad = (out_grad.astype(jnp.float32) * gelu_slope(pre_act.astype(jnp.float32))).astype(
        jnp.bfloat16
    )
    grad_all = lax.all_gather(hidden_grad, "row", axis=0, tiled=True)
    partial_value = lax.dot_general(
        grad_all, weight, (((1,), (1,)), ((), ())), preferred_element_type=jnp.float32
    )
    weight_sum = lax.dot_general(
        x_all, grad_all, (((0,), (0,)), ((), ())), preferred_element_type=jnp.float32
    )
    input_grad = lax.psum_scatter(partial_value, "col", scatter_dimension=0, tiled=True).astype(
        jnp.bfloat16
    )
    scale = 1.0 / (BLOCK * num_tokens)
    tiles = weight_sum.reshape(rows_here // BLOCK, BLOCK, cols_here // BLOCK, BLOCK)
    left = jnp.einsum("ipjq,irjq->ipjr", tiles, tiles, precision=lax.Precision.HIGHEST) * scale
    right = jnp.einsum("ipjq,ipjr->iqjr", tiles, tiles, precision=lax.Precision.HIGHEST) * scale
    left_stats = left.reshape(rows_here, cols_here).astype(jnp.bfloat16)
    right_stats = right.reshape(rows_here, cols_here).astype(jnp.bfloat16)
    return (input_grad, weight_sum.astype(jnp.bfloat16), left_stats, right_stats)


def solution(mesh):
    in_specs = (P("col", "row"), P("row", "col"), P("row", "col"), P("row", "col"))
    out_specs = (P("col", "row"), P("row", "col"), P("row", "col"), P("row", "col"))
    return jax.shard_map(
        on_device, mesh=mesh, in_specs=in_specs, out_specs=out_specs, check_vma=False
    )
```

profile of v0, /device:TPU:4, one launch (start us, length us, event | category | flops | bytes accessed | tf_op | source)
XLA Modules:
  0.0 233.7 jit_solution(4617175206382753291)
XLA Ops:
  7.2 0.0 copy-start
  7.2 0.0 all-gather.3.cloned.1.call-start
  7.2 2.6 %fusion.7 = bf16[64,3072]{1,0:T(8,128)(2,1)} fusion(bf16[64,3072]{1,0:T(8,128)(2,1)} %param.6, bf16[64,3072]{1,0:T(8,128)(2,1)} %param.7), kind=kLoop, calls=%fused_computation.17 | loop fusion | flops 4128768 | bytes 1179648 | tf_op jit(solution)/shard_map/convert_element_type | solution.py:24
  9.8 0.0 all-gather.3.cloned.1.call-update
  9.8 0.0 all-gather.5.cloned.1.call-start
  9.9 0.7 all-gather.5.cloned.1.call-update
  10.6 0.0 reduce-scatter.2.cloned.1.call-start
  10.6 118.4 %all-gather.3.cloned.1.call-done = bf16[2048,3072]{1,0:T(8,128)(2,1)} async-done(((bf16[64,3072]{1,0:T(8,128)(2,1)}), bf16[2048,3072]{1,0:T(8,128)(2,1)}) %all-gather.3.cloned.1.call-update) | async-done | bytes 12582928 | tf_op jit(solution)/shard_map/all_gather | solution.py:27
  129.0 0.0 copy-done
  129.0 10.8 %fusion.9 = f32[2048,384]{1,0:T(8,128)} fusion(bf16[2048,3072]{1,0:T(8,128)(2,1)} %all-gather.3.cloned.1.call-done, bf16[384,3072]{1,0:T(8,128)(2,1)S(1)} %copy-done), kind=kOutput, calls=%fused_computation.19 | convolution fusion | flops 4831838208 | bytes 18087936 | tf_op jit(solution)/shard_map/dot_general | solution.py:28
  139.8 0.0 reduce-scatter.2.cloned.1.call-update
  139.8 32.6 %all-gather.5.cloned.1.call-done = bf16[2048,384]{1,0:T(8,128)(2,1)} async-done(((bf16[256,384]{1,0:T(8,128)(2,1)}), bf16[2048,384]{1,0:T(8,128)(2,1)}) %all-gather.5.cloned.1.call-update) | async-done | bytes 1572880 | tf_op jit(solution)/shard_map/all_gather | solution.py:20
  172.4 12.1 %bitcast_convert_fusion = (bf16[384,3072]{0,1:T(8,128)(2,1)}, f32[3072,384]{1,0:T(8,128)}) fusion(bf16[2048,3072]{1,0:T(8,128)(2,1)} %all-gather.3.cloned.1.call-done, bf16[2048,384]{1,0:T(8,128)(2,1)} %all-gather.5.cloned.1.call-done), kind=kOutput, calls=%fused_computation | convolution fusion | flops 4833017856 | bytes 21233664 | tf_op jit(solution)/shard_map/dot_general | solution.py:31
  184.5 4.3 %copy.11 = bf16[384,3072]{1,0:T(8,128)(2,1)} copy(bf16[384,3072]{0,1:T(8,128)(2,1)} %get-tuple-element.8) | data formatting | bytes 4718592
  188.7 14.0 %multiply_convert_fusion.1 = bf16[8,384,384]{2,1,0:T(8,128)(2,1)} fusion(f32[384,8,384]{0,2,1:T(8,128)} %bitcast.22), kind=kOutput, calls=%fused_computation.2 | convolution fusion | flops 5438177280 | bytes 7077888 | tf_op jit(solution)/shard_map/ipjq,irjq->ipjr/dot_general | solution.py:39
  202.8 4.3 %copy.12 = bf16[384,3072]{1,0:T(8,128)(2,1)} copy(bf16[384,3072]{0,1:T(8,128)(2,1)} %bitcast.25) | data formatting | bytes 4718592
  207.0 14.2 %multiply_convert_fusion = bf16[8,384,384]{2,1,0:T(8,128)(2,1)} fusion(f32[384,8,384]{0,2,1:T(8,128)} %bitcast.23), kind=kOutput, calls=%fused_computation.1 | convolution fusion | flops 5438177280 | bytes 7077888 | tf_op jit(solution)/shard_map/ipjq,ipjr->iqjr/dot_general | solution.py:40
  221.2 4.3 %copy.13 = bf16[384,3072]{1,0:T(8,128)(2,1)} copy(bf16[384,3072]{0,1:T(8,128)(2,1)} %bitcast.24) | data formatting | bytes 4718592
  225.5 0.0 reduce-scatter.2.cloned.1.call-done
  225.5 1.7 convert_element_type.42
Async XLA Ops:
  7.2 121.8 %copy-start = (bf16[384,3072]{1,0:T(8,128)(2,1)S(1)}, bf16[384,3072]{1,0:T(8,128)(2,1)}, u32[]{:S(2)}) copy-start(bf16[384,3072]{1,0:T(8,128)(2,1)} %param.5) | copy-start | bytes 7077892
  7.2 121.8 %all-gather.3.cloned.1.call-start = ((), (), s32[]{:S(2)}) async-start(), calls=%async_computation.1 | async-start | bytes 12976128 | tf_op jit(solution)/shard_map/all_gather | solution.py:27
  9.8 162.6 %all-gather.5.cloned.1.call-start = ((), (), s32[]{:S(2)}) async-start(), calls=%async_computation.3 | async-start | bytes 1769472 | tf_op jit(solution)/shard_map/all_gather | solution.py:20
  10.6 215.0 %reduce-scatter.2.cloned.1.call-start = ((), (), s32[]{:S(2)}) async-start(), calls=%async_computation.2 | async-start | bytes 3538944 | tf_op jit(solution)/shard_map/reduce_scatter | solution.py:34
Sparse Core Ops, SparseCore 0:
  11.3 117.6 all-gather.2
  130.8 41.5 all-gather.4
  175.0 48.3 reduce-scatter.1
where the time goes:
time: 234 us
  waiting for transfers between devices  152 us (65%)
  matrix products  51.1 us (22%)
  between operations  13.8 us (6%)
  local copies, waits for them, and re-layouts  12.8 us (5%)
  other arithmetic  4.26 us (2%)
    all_gather x1, waiting for transfers between devices, on_device(): grad_all = lax.all_gather(hidden_grad, 'row', axis=0, tiled=True)  118 us
    all_gather x1, waiting for transfers between devices, on_device(): x_all = lax.all_gather(tokens, 'col', axis=0, tiled=True)  32.6 us
    dot_general x1, matrix products, on_device(): jnp.einsum('ipjq,ipjr->iqjr', tiles, tiles, precision=lax.Precision.HIGHEST)  14.2 us
    dot_general x1, matrix products, on_device(): jnp.einsum('ipjq,irjq->ipjr', tiles, tiles, precision=lax.Precision.HIGHEST)  14 us
    unnamed x5, local copies, waits for them, and re-layouts  12.8 us
    dot_general x1, matrix products, on_device(): lax.dot_general(x_all, grad_all, (((0,), (0,)), ((), ())), preferred_elem...  12.1 us
    dot_general x1, matrix products, on_device(): lax.dot_general(grad_all, weight, (((1,), (1,)), ((), ())), preferred_ele...  10.8 us
  transfers between devices with their start and end apart: 3, of which 2 were waited for; matrix products, arithmetic and copies ran while one was open for 27% of the time, Pallas kernels for 0%

commit v1 on v0

--- a/solution.py
+++ b/solution.py
@@ -24,7 +24,10 @@
     hidden_grad = (out_grad.astype(jnp.float32) * gelu_slope(pre_act.astype(jnp.float32))).astype(
         jnp.bfloat16
     )
-    grad_all = lax.all_gather(hidden_grad, "row", axis=0, tiled=True)
+    count = lax.axis_size("row")
+    blocks = jnp.stack([hidden_grad for _ in range(count)])
+    blocks = lax.all_to_all(blocks, "row", split_axis=0, concat_axis=0)
+    grad_all = jnp.concatenate(blocks, axis=0)
     partial_value = lax.dot_general(
         grad_all, weight, (((1,), (1,)), ((), ())), preferred_element_type=jnp.float32
     )

time: 234 us -> 371 us (1.59)
  waiting for transfers between devices: 152 us -> 275 us
  starting transfers between devices: 0.12 us -> 11.7 us
  local copies, waits for them, and re-layouts: 12.8 us -> 18.9 us
  matrix products: 51.1 us -> 47.3 us
    all_to_all x0 -> x1, waiting for transfers between devices: none -> 274 us  [on_device(): blocks = lax.all_to_all(blocks, 'row', split_axis=0, concat_axis=0)]
    all_gather x1 -> x0, waiting for transfers between devices: 118 us -> none  [on_device(): grad_all = lax.all_gather(hidden_grad, 'row', axis=0, tiled=True)]
    all_gather x1, waiting for transfers between devices: 32.6 us -> 0.02 us  [on_device(): x_all = lax.all_gather(tokens, 'col', axis=0, tiled=True)]
    all_to_all x0 -> x1, starting transfers between devices: none -> 11.6 us  [on_device(): blocks = lax.all_to_all(blocks, 'row', split_axis=0, concat_axis=0)]
    another operation x0 -> x1, local copies, waits for them, and re-layouts: none -> 6.08 us  [on_device(): blocks = jnp.stack([hidden_grad for _ in range(count)])]
    unnamed x5 -> x7, local copies, waits for them, and re-layouts: 12.8 us -> 12.8 us
  transfers between devices with their start and end apart: 3 -> 3, of which waited for: 2 -> 1; matrix products, arithmetic and copies ran while one was open for 27% -> 16% of each run, Pallas kernels for 0% -> 0%
where the time goes in v1:
time: 371 us; the launch traced here: 370 us
  waiting for transfers between devices  275 us (74%)
  matrix products  47.3 us (13%)
  local copies, waits for them, and re-layouts  18.9 us (5%)
  between operations  14.1 us (4%)
  starting transfers between devices  11.7 us (3%)
    all_to_all x1, waiting for transfers between devices, on_device(): blocks = lax.all_to_all(blocks, 'row', split_axis=0, concat_axis=0)  274 us
    dot_general x1, matrix products, on_device(): jnp.einsum('ipjq,ipjr->iqjr', tiles, tiles, precision=lax.Precision.HIGHEST)  14 us
    unnamed x7, local copies, waits for them, and re-layouts  12.8 us
    all_to_all x1, starting transfers between devices, on_device(): blocks = lax.all_to_all(blocks, 'row', split_axis=0, concat_axis=0)  11.6 us
    dot_general x1, matrix products, on_device(): lax.dot_general(x_all, grad_all, (((0,), (0,)), ((), ())), preferred_elem...  11.3 us
    dot_general x1, matrix products, on_device(): jnp.einsum('ipjq,irjq->ipjr', tiles, tiles, precision=lax.Precision.HIGHEST)  11.2 us
    dot_general x1, matrix products, on_device(): lax.dot_general(grad_all, weight, (((1,), (1,)), ((), ())), preferred_ele...  10.8 us
  transfers between devices with their start and end apart: 3, of which 1 were waited for; matrix products, arithmetic and copies ran while one was open for 16% of the time, Pallas kernels for 0%

profile of v1, /device:TPU:4, one launch (start us, length us, event | category | flops | bytes accessed | tf_op | source)
XLA Modules:
  0.0 370.4 jit_solution(9259590298631019683)
XLA Ops:
  7.2 0.0 copy-start
  7.2 1.8 fusion.7
  9.0 6.1 %stack.2 = bf16[32,64,3072]{2,1,0:T(8,128)(2,1)} broadcast(bf16[64,3072]{1,0:T(8,128)(2,1)S(1)} %fusion.7), dimensions={1,2} | broadcast | bytes 12976128 | tf_op jit(solution)/shard_map/stack | solution.py:28
  15.1 11.6 %all-to-all-start = ((bf16[32,64,3072]{2,1,0:T(8,128)(2,1)}), bf16[32,64,3072]{2,1,0:T(8,128)(2,1)}, u32[]{:S(2)}, u32[]{:S(2)}) async-start(bf16[32,64,3072]{2,1,0:T(8,128)(2,1)} %stack.2), calls=%async_computation | async-start | bytes 25165824 | tf_op jit(solution)/shard_map/all_to_all | solution.py:29
  26.7 0.0 all-gather.2.cloned.1.call-start
  26.8 0.7 all-gather.2.cloned.1.call-update
  27.5 0.0 reduce-scatter.2.cloned.1.call-start
  27.5 274.2 %all-to-all-done = bf16[32,64,3072]{2,1,0:T(8,128)(2,1)} async-done(((bf16[32,64,3072]{2,1,0:T(8,128)(2,1)}), bf16[32,64,3072]{2,1,0:T(8,128)(2,1)}, u32[]{:S(2)}, u32[]{:S(2)}) %all-to-all-start) | async-done | bytes 12582944 | tf_op jit(solution)/shard_map/all_to_all | solution.py:29
  301.7 0.0 copy-done
  301.7 10.8 %fusion.9 = f32[2048,384]{1,0:T(8,128)} fusion(bf16[2048,3072]{1,0:T(8,128)(2,1)} %bitcast, bf16[384,3072]{1,0:T(8,128)(2,1)S(1)} %copy-done), kind=kOutput, calls=%fused_computation.19 | convolution fusion | flops 4831838208 | bytes 18087936 | tf_op jit(solution)/shard_map/dot_general | solution.py:31
  312.5 0.0 reduce-scatter.2.cloned.1.call-update
  312.5 0.0 all-gather.2.cloned.1.call-done
  312.5 11.3 %bitcast_convert_fusion = (bf16[384,3072]{0,1:T(8,128)(2,1)}, f32[3072,384]{1,0:T(8,128)S(1)}) fusion(bf16[2048,3072]{1,0:T(8,128)(2,1)} %bitcast, bf16[2048,384]{1,0:T(8,128)(2,1)} %all-gather.2.cloned.1.call-done), kind=kOutput, calls=%fused_computation | convolution fusion | flops 4833017856 | bytes 21233664 | tf_op jit(solution)/shard_map/dot_general | solution.py:34
  323.8 0.0 copy-start.1
  323.8 11.2 %multiply_convert_fusion.1 = bf16[8,384,384]{2,1,0:T(8,128)(2,1)} fusion(f32[384,8,384]{0,2,1:T(8,128)S(1)} %bitcast.23), kind=kOutput, calls=%fused_computation.2 | convolution fusion | flops 5438177280 | bytes 7077888 | tf_op jit(solution)/shard_map/ipjq,irjq->ipjr/dot_general | solution.py:42
  335.0 0.0 copy-done.1
  335.0 4.3 %copy.12 = bf16[384,3072]{1,0:T(8,128)(2,1)} copy(bf16[384,3072]{0,1:T(8,128)(2,1)} %bitcast.26) | data formatting | bytes 4718592
  339.3 14.0 %multiply_convert_fusion = bf16[8,384,384]{2,1,0:T(8,128)(2,1)} fusion(f32[384,8,384]{0,2,1:T(8,128)} %bitcast.24), kind=kOutput, calls=%fused_computation.1 | convolution fusion | flops 5438177280 | bytes 7077888 | tf_op jit(solution)/shard_map/ipjq,ipjr->iqjr/dot_general | solution.py:43
  353.3 4.3 %copy.13 = bf16[384,3072]{1,0:T(8,128)(2,1)} copy(bf16[384,3072]{0,1:T(8,128)(2,1)} %bitcast.25) | data formatting | bytes 4718592
  357.6 4.3 %copy.11 = bf16[384,3072]{1,0:T(8,128)(2,1)} copy(bf16[384,3072]{0,1:T(8,128)(2,1)} %get-tuple-element.8) | data formatting | bytes 4718592
  361.9 0.0 reduce-scatter.2.cloned.1.call-done
  361.9 1.7 convert_element_type.42
Async XLA Ops:
  7.2 294.5 %copy-start = (bf16[384,3072]{1,0:T(8,128)(2,1)S(1)}, bf16[384,3072]{1,0:T(8,128)(2,1)}, u32[]{:S(2)}) copy-start(bf16[384,3072]{1,0:T(8,128)(2,1)} %param.5) | copy-start | bytes 7077892
  15.1 286.6 %all-to-all-start = ((bf16[32,64,3072]{2,1,0:T(8,128)(2,1)}), bf16[32,64,3072]{2,1,0:T(8,128)(2,1)}, u32[]{:S(2)}, u32[]{:S(2)}) async-start(bf16[32,64,3072]{2,1,0:T(8,128)(2,1)} %stack.2), calls=%async_computation | async-start | bytes 25165824 | tf_op jit(solution)/shard_map/all_to_all | solution.py:29
  26.7 285.8 %all-gather.2.cloned.1.call-start = ((), (), s32[]{:S(2)}) async-start(), calls=%async_computation.3 | async-start | bytes 1769472 | tf_op jit(solution)/shard_map/all_gather | solution.py:20
  27.5 334.4 %reduce-scatter.2.cloned.1.call-start = ((), (), s32[]{:S(2)}) async-start(), calls=%async_computation.2 | async-start | bytes 3538944 | tf_op jit(solution)/shard_map/reduce_scatter | solution.py:37
  323.8 11.2 %copy-start.1 = (f32[3072,384]{1,0:T(8,128)}, f32[3072,384]{1,0:T(8,128)S(1)}, u32[]{:S(2)}) copy-start(f32[3072,384]{1,0:T(8,128)S(1)} %get-tuple-element.9) | copy-start | bytes 14155780
Sparse Core Ops, SparseCore 0:
  29.3 58.1 all-gather.1
  312.6 47.4 reduce-scatter.1
